TPU v7x, 32 devices: a whole 2x2x4 slice. The times are simulated.
32 devices in a mesh: bra: 8 (over z, y), ket: 4 (over x, core).
Axes of the slice: x: 2, y: 2, z: 4, core: 2. Of those that a mesh axis runs over, the one named last changes fastest.
Arguments:
- integrals: bfloat16 [256, 1024, 1024], P(('bra', 'ket')), may hold values from -0.1875 to 0.1875
- quartets: int32 [256, 4], P(('bra', 'ket')), may hold values from 0 to 127, as said below
- density: bfloat16 [128, 128, 12, 1024], P(('bra', 'ket')), may hold values from -6 to 6
- owner_map: int32 [128], replicated, may hold values from 0 to 127, each once
Outputs:
- fock_rows: bfloat16 [128, 128, 12, 1024], P(('bra', 'ket'))
Inputs may be any that keep to these rules, and one draw needn't show every extreme that they name: `quartets`: the 32 block indices in the 8 rows of one device are distinct, and one block index is the first entry of some row on every device. Block row X of density and of fock_rows is stored at row owner_map[X]; each device holds 4 consecutive storage rows, in device order.
All inputs are finite; a program needn't handle non-finite values.
Results may differ from a plain program's by a relative error of at most 0.001.
Values may be sent and summed in bfloat16 or wider, within the bound.
No kernel may reach another device: no remote copies, remote signals or barrier semaphores. Data moves between devices by JAX's collectives and lax.ppermute only.
A program may use at most 384 MiB of HBM per device.

v0:
```python
import math

import jax
import jax.numpy as jnp
from jax import lax
from jax.sharding import PartitionSpec as P

ROLE_ROW = (0, 0, 1, 1, 2, 3)
ROLE_COL = (1, 2, 2, 3, 3, 0)


def contract_all(integrals, read_tiles):
    quartet_count = integrals.shape[0]
    width = math.isqrt(integrals.shape[1])
    split_blocks = integrals.reshape(quartet_count, width, width, width, width)
    pr_layout = jnp.transpose(split_blocks, (0, 1, 3, 2, 4)).reshape(
        quartet_count, width * width, width * width
    )
    qr_layout = jnp.transpose(split_blocks, (0, 2, 3, 4, 1)).reshape(
        quartet_count, width * width, width * width
    )
    term_zero = 2.0 * jnp.einsum(
        "iab,inb->ina", integrals, read_tiles[:, 4], preferred_element_type=jnp.float32
    )
    term_four = 2.0 * jnp.einsum(
        "iab,ina->inb", integrals, read_tiles[:, 0], preferred_element_type=jnp.float32
    )
    term_one = -jnp.einsum(
        "iab,inb->ina", pr_layout, read_tiles[:, 3], preferred_element_type=jnp.float32
    )
    term_three = -jnp.einsum(
        "iab,ina->inb", pr_layout, read_tiles[:, 1], preferred_element_type=jnp.float32
    )
    term_two = -jnp.einsum(
        "iab,inb->ina", qr_layout, read_tiles[:, 5], preferred_element_type=jnp.float32
    )
    term_five = -jnp.einsum(
        "iab,ina->inb", qr_layout, read_tiles[:, 2], preferred_element_type=jnp.float32
    )
    return jnp.stack([term_zero, term_one, term_two, term_three, term_four, term_five], axis=1)


def tile_slots(quartets, owner_map, rows_dev, peer_most):
    blocks_total = owner_map.shape[0]
    lead_shape = quartets.shape[:-2]
    row_blocks = jnp.stack([quartets[..., column_pick] for column_pick in ROLE_ROW], -1).reshape(
        lead_shape + (-1,)
    )
    col_blocks = jnp.stack([quartets[..., column_pick] for column_pick in ROLE_COL], -1).reshape(
        lead_shape + (-1,)
    )
    block_ids = jnp.arange(blocks_total, dtype=jnp.int32)
    storage = jnp.sum(jnp.where(row_blocks[..., None] == block_ids, owner_map, 0), axis=-1)
    target = storage // rows_dev
    local_tile = storage % rows_dev * blocks_total + col_blocks
    need_count = target.shape[-1]
    positions = jnp.arange(need_count)
    earlier = (target[..., None, :] == target[..., :, None]) & (
        positions[None, :] < positions[:, None]
    )
    slot_rank = jnp.sum(earlier.astype(jnp.int32), axis=-1)
    return (target, slot_rank, target * peer_most + slot_rank, local_tile)


def local(integrals, quartets, density, owner_map):
    rows_dev, blocks_total, dens_count, tile_len = density.shape
    devices = lax.axis_size(("bra", "ket"))
    peer_most = 2 * rows_dev
    slot_count = devices * peer_most
    quartet_count = quartets.shape[0]
    target, slot_rank, slot_index, local_tile = tile_slots(quartets, owner_map, rows_dev, peer_most)
    slot_ids = jnp.arange(slot_count)
    slot_hit = slot_index[None, :] == slot_ids[:, None]
    requests = jnp.sum(jnp.where(slot_hit, local_tile[None, :] + 1, 0), axis=1) - 1
    incoming = lax.all_to_all(
        requests.reshape(devices, peer_most),
        ("bra", "ket"),
        split_axis=0,
        concat_axis=0,
        tiled=True,
    )
    is_live = incoming >= 0
    flat_density = density.reshape(rows_dev * blocks_total, dens_count, tile_len)
    picked = flat_density[jnp.maximum(incoming, 0)]
    picked = jnp.where(is_live[:, :, None, None], picked, jnp.zeros((), jnp.bfloat16))
    returned = lax.all_to_all(picked, ("bra", "ket"), split_axis=0, concat_axis=0, tiled=True)
    read_tiles = returned.reshape(slot_count, dens_count, tile_len)[slot_index].reshape(
        quartet_count, 6, dens_count, tile_len
    )
    contributions = contract_all(integrals, read_tiles)
    outgoing = (
        jnp.zeros((slot_count, dens_count, tile_len), jnp.float32)
        .at[slot_index]
        .set(contributions.reshape(quartet_count * 6, dens_count, tile_len))
    )
    arrived = lax.all_to_all(
        outgoing.reshape(devices, peer_most, dens_count, tile_len),
        ("bra", "ket"),
        split_axis=0,
        concat_axis=0,
        tiled=True,
    )
    destination = jnp.where(is_live, incoming, rows_dev * blocks_total).reshape(-1)
    fock_rows = (
        jnp.zeros((rows_dev * blocks_total, dens_count, tile_len), jnp.float32)
        .at[destination]
        .add(arrived.reshape(slot_count, dens_count, tile_len), mode="drop")
    )
    return fock_rows.reshape(rows_dev, blocks_total, dens_count, tile_len).astype(jnp.bfloat16)


def solution(mesh):
    return jax.shard_map(
        local,
        mesh=mesh,
        in_specs=(
            P(("bra", "ket"), None, None),
            P(("bra", "ket"), None),
            P(("bra", "ket"), None, None, None),
            P(),
        ),
        out_specs=P(("bra", "ket"), None, None, None),
        check_vma=False,
    )
```

profile of v0, /device:TPU:0, one launch (start us, length us, event | category | flops | bytes accessed | tf_op | source)
XLA Modules:
  0.0 997.8 jit_solution(15366847854970366720)
XLA Ops:
  4.8 7.3 all-to-all-start
  18.4 28.2 %copy.130 = bf16[512,12,1024]{2,1,0:T(8,128)(2,1)} copy(bf16[512,12,1024]{2,0,1:T(8,128)(2,1)S(1)} %bitcast.102) | data formatting | bytes 25165824 | tf_op jit(solution)/shard_map/reshape | solution.py:83
  47.0 14.3 %gather_fusion = bf16[256,12,1024]{2,1,0:T(8,128)(2,1)} fusion(bf16[512,12,1024]{2,1,0:T(8,128)(2,1)} %copy.130, s32[1024]{0:T(1024)S(1)} %pad_clamp_fusion.1), kind=kCustom, calls=%fused_computation | custom fusion | bytes 12583936 | tf_op jit(solution)/shard_map/gather | solution.py:84
  61.3 9.7 copy_select_fusion
  77.3 77.0 %reshape.216 = bf16[8,32,32,32,32]{4,3,2,1,0:T(8,128)(2,1)} reshape(bf16[8,1024,1024]{2,1,0:T(8,128)(2,1)} %param.4) | data formatting | bytes 33554432 | tf_op jit(solution)/shard_map/reshape | solution.py:15
  154.3 44.3 %copy.136 = bf16[8,32,32,32,32]{4,3,2,1,0:T(8,128)(2,1)} copy(bf16[8,32,32,32,32]{4,2,3,1,0:T(8,128)(2,1)} %bitcast.13) | data formatting | bytes 33554432 | tf_op jit(solution)/shard_map/transpose | solution.py:16
  198.6 88.6 %reshape.217 = bf16[8,1024,1024]{2,1,0:T(8,128)(2,1)} reshape(bf16[8,32,32,32,32]{4,3,2,1,0:T(8,128)(2,1)} %copy.136) | data formatting | bytes 33554432 | tf_op jit(solution)/shard_map/reshape | solution.py:16
  287.2 98.3 %copy.138 = bf16[8,32,32,32,32]{4,3,2,1,0:T(8,128)(2,1)} copy(bf16[8,32,32,32,32]{3,2,1,4,0:T(8,128)(2,1)} %bitcast.16) | data formatting | bytes 33554432 | tf_op jit(solution)/shard_map/transpose | solution.py:19
  385.5 88.6 %reshape.218 = bf16[8,1024,1024]{2,1,0:T(8,128)(2,1)} reshape(bf16[8,32,32,32,32]{4,3,2,1,0:T(8,128)(2,1)} %copy.138) | data formatting | bytes 33554432 | tf_op jit(solution)/shard_map/reshape | solution.py:19
  474.1 11.6 %copy.132 = bf16[32,8,12,1024]{3,2,1,0:T(8,128)(2,1)} copy(bf16[32,8,12,1024]{3,1,2,0:T(8,128)(2,1)} %all-to-all-done.1) | data formatting | bytes 12582912 | tf_op jit(solution)/shard_map/all_to_all | solution.py:86
  489.8 11.0 %fusion.11 = f32[8,6,12,1024]{3,2,0,1:T(8,128)} fusion(bf16[8,1024,1024]{2,1,0:T(8,128)(2,1)} %param.4, bf16[8,6,12,1024]{3,2,1,0:T(8,128)(2,1)S(1)} %bitcast.107), kind=kOutput, calls=%fused_computation.24 | convolution fusion | flops 201424896 | bytes 17563648 | tf_op jit(solution)/shard_map/iab,inb->ina/dot_general | solution.py:22
  500.8 11.2 %fusion.7 = f32[8,6,12,1024]{3,2,0,1:T(8,128)} fusion(f32[8,6,12,1024]{3,2,0,1:T(8,128)} %fusion.11, bf16[8,1024,1024]{2,1,0:T(8,128)(2,1)} %reshape.217, bf16[8,6,12,1024]{3,2,1,0:T(8,128)(2,1)S(1)} %bitcast.108), kind=kOutput, calls=%fused_computation.18 | convolution fusion | flops 201424896 | bytes 17563648 | tf_op jit(solution)/shard_map/iab,inb->ina/dot_general | solution.py:28
  512.0 11.0 %fusion.5 = f32[8,6,12,1024]{3,2,0,1:T(8,128)} fusion(f32[8,6,12,1024]{3,2,0,1:T(8,128)} %fusion.7, bf16[8,1024,1024]{2,1,0:T(8,128)(2,1)} %reshape.218, bf16[8,6,12,1024]{3,2,1,0:T(8,128)(2,1)S(1)} %bitcast.109), kind=kOutput, calls=%fused_computation.15 | convolution fusion | flops 201424896 | bytes 17563648 | tf_op jit(solution)/shard_map/iab,inb->ina/dot_general | solution.py:34
  523.0 9.0 fusion.3
  532.0 9.0 fusion.9
  546.3 8.1 broadcast_in_dim.61
  554.4 7.9 scatter_fusion
  562.2 23.2 %copy.144 = f32[32,8,12,1024]{3,1,2,0:T(8,128)} copy(f32[32,8,12,1024]{3,2,1,0:T(8,128)} %bitcast.100) | data formatting | bytes 25165824 | tf_op jit(solution)/shard_map/reshape | solution.py:97
  592.7 277.1 %all-to-all-done.2 = f32[32,8,12,1024]{3,1,2,0:T(8,128)} async-done(((f32[32,8,12,1024]{3,1,2,0:T(8,128)}), f32[32,8,12,1024]{3,1,2,0:T(8,128)}, u32[]{:S(2)}, u32[]{:S(2)}) %all-to-all-start.2) | async-done | bytes 12582944 | tf_op jit(solution)/shard_map/all_to_all | solution.py:96
  869.8 12.1 %copy.168 = f32[32,8,12,1024]{3,1,0,2:T(8,128)} copy(f32[32,8,12,1024]{3,1,2,0:T(8,128)} %all-to-all-done.2) | data formatting | bytes 25165824 | tf_op jit(solution)/shard_map/all_to_all | solution.py:96
  881.9 17.8 %copy.146 = f32[256,12,1024]{2,1,0:T(8,128)} copy(f32[256,12,1024]{2,0,1:T(8,128)} %bitcast.101) | data formatting | bytes 25165824 | tf_op jit(solution)/shard_map/reshape | solution.py:107
  899.7 11.3 %broadcast_in_dim.55 = f32[512,12,1024]{2,1,0:T(8,128)} broadcast(f32[]{:T(128)} %constant.18.clone.1), dimensions={} | broadcast | bytes 25165828 | tf_op jit(solution)/shard_map/broadcast_in_dim | solution.py:105
  911.0 57.0 %scatter_fusion.1 = f32[512,12,1024]{2,1,0:T(8,128)} fusion(f32[512,12,1024]{2,1,0:T(8,128)} %broadcast_in_dim.55, s32[256]{0:T(256)S(1)} %bitcast.113, f32[256,12,1024]{2,1,0:T(8,128)} %copy.146), kind=kCustom, calls=%fused_computation.3 | custom fusion | flops 3145728 | bytes 37749760 | tf_op jit(solution)/shard_map/scatter-add | solution.py:107
  967.9 24.3 %copy.167 = bf16[512,12,1024]{2,0,1:T(8,128)(2,1)S(1)} copy(f32[512,12,1024]{2,1,0:T(8,128)} %scatter_fusion.1) | data formatting | bytes 37748736 | tf_op jit(solution)/shard_map/scatter-add | solution.py:107
  (58 shorter events, 39.8 us)
Async XLA Ops:
  3.4 0.5 copy-start.2
  3.6 0.5 copy-start.4
  4.8 41.8 %all-to-all-start = ((s32[32,1,8]{2,1,0:T(1,128)}), s32[32,1,8]{2,1,0:T(1,128)S(1)}, u32[]{:S(2)}, u32[]{:S(2)}) async-start(s32[32,1,8]{2,1,0:T(1,128)} %bitcast), calls=%async_computation | async-start | bytes 32768 | tf_op jit(solution)/shard_map/all_to_all | solution.py:75
  46.6 14.6 %copy-start = (s32[32,1,8]{2,1,0:T(1,128)}, s32[32,1,8]{2,1,0:T(1,128)S(1)}, u32[]{:S(2)}) copy-start(s32[32,1,8]{2,1,0:T(1,128)S(1)} %all-to-all-done) | copy-start | bytes 3076
  70.9 403.2 %all-to-all-start.1 = ((bf16[32,8,12,1024]{3,1,2,0:T(8,128)(2,1)}), bf16[32,8,12,1024]{3,1,2,0:T(8,128)(2,1)}, u32[]{:S(2)}, u32[]{:S(2)}) async-start(bf16[32,8,12,1024]{3,1,2,0:T(8,128)(2,1)} %copy_select_fusion), calls=%async_computation.1 | async-start | bytes 12582912 | tf_op jit(solution)/shard_map/all_to_all | solution.py:86
  385.5 88.6 %copy-start.3 = (s32[48]{0:T(128)S(1)}, s32[48]{0:T(128)}, u32[]{:S(2)}) copy-start(s32[48]{0:T(128)} %copy-done.2) | copy-start | bytes 580
  385.5 88.6 %copy-start.5 = (s32[48]{0:T(128)S(1)}, s32[48]{0:T(128)}, u32[]{:S(2)}) copy-start(s32[48]{0:T(128)} %copy-done.4) | copy-start | bytes 580
  523.0 18.0 %slice-start = ((s8[16777216]{0:T(1024)(128)(4,1)}), s8[4194304]{0:T(1024)(128)(4,1)S(1)}, s32[]{:S(2)}) async-start(s8[16777216]{0:T(1024)(128)(4,1)} %bitcast.98), calls=%async_computation.3 | async-start | bytes 8388608
  523.0 18.0 %slice-start.1 = ((s8[16777216]{0:T(1024)(128)(4,1)}), s8[4194304]{0:T(1024)(128)(4,1)S(1)}, s32[]{:S(2)}) async-start(s8[16777216]{0:T(1024)(128)(4,1)} %bitcast.98), calls=%async_computation.4 | async-start | bytes 8388608
  532.0 9.0 slice-start.2
  532.0 9.0 slice-start.3
  585.4 6.5 copy-start.1
  585.4 284.4 %all-to-all-start.2 = ((f32[32,8,12,1024]{3,1,2,0:T(8,128)}), f32[32,8,12,1024]{3,1,2,0:T(8,128)}, u32[]{:S(2)}, u32[]{:S(2)}) async-start(f32[32,8,12,1024]{3,1,2,0:T(8,128)} %copy.144), calls=%async_computation.2 | async-start | bytes 25165824 | tf_op jit(solution)/shard_map/all_to_all | solution.py:96
where the time goes:
time: 1020 us; the launch traced here: 998 us
  local copies, waits for them, and re-layouts  578 us (57%)
  waiting for transfers between devices  277 us (27%)
  other arithmetic  68.5 us (7%)
  matrix products  54.3 us (5%)
  starting transfers between devices  19.7 us (2%)
    all_to_all x1, waiting for transfers between devices, local(): lax.all_to_all(outgoing.reshape(devices, peer_most, dens_count, tile_len)...  277 us
    transpose x1, local copies, waits for them, and re-layouts, contract_all(): jnp.transpose(split_blocks, (0, 2, 3, 4, 1))  98.3 us
    reshape x1, local copies, waits for them, and re-layouts, contract_all(): jnp.transpose(split_blocks, (0, 1, 3, 2, 4))  88.6 us
    reshape x1, local copies, waits for them, and re-layouts, contract_all(): jnp.transpose(split_blocks, (0, 2, 3, 4, 1))  88.6 us
    reshape x1, local copies, waits for them, and re-layouts, contract_all(): split_blocks = integrals.reshape(quartet_count, width, width, width, width)  77 us
    scatter-add x1, other arithmetic, local(): fock_rows = jnp.zeros((rows_dev * blocks_total, dens_count, tile_len), jn...  57 us
    transpose x1, local copies, waits for them, and re-layouts, contract_all(): jnp.transpose(split_blocks, (0, 1, 3, 2, 4))  44.3 us
    reshape x1, local copies, waits for them, and re-layouts, local(): density.reshape(rows_dev * blocks_total, dens_count, tile_len)  28.2 us
  transfers between devices with their start and end apart: 3, of which 1 were waited for; matrix products, arithmetic and copies ran while one was open for 43% of the time, Pallas kernels for 0%

commit v1 on v0

v1 whole, which is shorter than its diff:
```python
import functools
import math

import jax
import jax.numpy as jnp
from jax import lax
from jax.experimental import pallas as pl
from jax.experimental.pallas import tpu as pltpu
from jax.sharding import PartitionSpec as P

ROLE_ROW = (0, 0, 1, 1, 2, 3)
ROLE_COL = (1, 2, 2, 3, 3, 0)
ROLES = 6
PAD_N = 16
ROWS = 16
AXES = ("bra", "ket")
BF16 = jnp.bfloat16
F32 = jnp.float32
VMEM_BYTES = 60 * 1024 * 1024


def params(axes=1):
    return pltpu.CompilerParams(
        dimension_semantics=("arbitrary",) * axes, vmem_limit_bytes=VMEM_BYTES
    )


def cost(flops, moved):
    return pl.CostEstimate(flops=int(flops), bytes_accessed=int(moved), transcendentals=0)


def hot_rows(target, width, base=0):
    columns = lax.broadcasted_iota(jnp.int32, (target.shape[0], width), 1) + base
    return jnp.where(columns == target, 1.0, 0.0).astype(BF16)


def hot_columns(target, height, base=0):
    rows = lax.broadcasted_iota(jnp.int32, (height, target.shape[1]), 0) + base
    return jnp.where(rows == target, 1.0, 0.0).astype(BF16)


def dot_nn(left, right):
    return jnp.dot(left, right, preferred_element_type=F32)


def dot_nt(left, right):
    return lax.dot_general(left, right, (((1,), (1,)), ((), ())), preferred_element_type=F32)


def gather_body(target_ref, density_ref, out_ref, hot_ref):
    peers, _, rows, lanes = out_ref.shape
    depth = hot_ref.shape[1]

    @pl.when(pl.program_id(0) == 0)
    def _():
        hot_ref[...] = hot_rows(target_ref[...], depth)

    source = density_ref[...].reshape(depth, lanes)
    half = lanes // 2
    for part in range(2):
        span = slice(part * half, (part + 1) * half)
        picked = dot_nn(hot_ref[...], source[:, span]).astype(BF16)
        out_ref[:, 0, :, span] = picked.reshape(peers, rows, half)


def gather_tiles(wanted, density_rows, slots):
    peers = wanted.shape[0]
    rows_dev, dens, blocks, lanes = density_rows.shape
    per = ROWS // slots
    groups = dens // per
    depth = rows_dev * per * blocks
    tile_row, tile_col = wanted // blocks, wanted % blocks
    inner = jnp.arange(per, dtype=jnp.int32)[None, :, None]
    target = tile_row[:, None, :] * (per * blocks) + inner * blocks + tile_col[:, None, :]
    target = jnp.where(wanted[:, None, :] >= 0, target, -1).reshape(peers * ROWS, 1)
    return pl.pallas_call(
        gather_body,
        grid=(groups,),
        in_specs=[
            pl.BlockSpec((peers * ROWS, 1), lambda g: (0, 0)),
            pl.BlockSpec((rows_dev, per, blocks, lanes), lambda g: (0, g, 0, 0)),
        ],
        out_specs=pl.BlockSpec((peers, 1, ROWS, lanes), lambda g: (0, g, 0, 0)),
        out_shape=jax.ShapeDtypeStruct((peers, groups, ROWS, lanes), BF16),
        scratch_shapes=[pltpu.VMEM((peers * ROWS, depth), BF16)],
        compiler_params=params(),
        name="gather_tiles",
    )(target, density_rows)


def select_body(target_ref, swap_ref, slots_ref, out_ref, total_ref):
    step = pl.program_id(0)
    depth, lanes = slots_ref.shape

    @pl.when(step == 0)
    def _():
        total_ref[...] = jnp.zeros_like(total_ref)

    total_ref[...] += dot_nn(hot_rows(target_ref[...], depth, step * depth), slots_ref[...])

    @pl.when(step == pl.num_programs(0) - 1)
    def _():
        span = out_ref.shape[0] // ROLES
        for role in range(ROLES):
            rows = slice(role * span, (role + 1) * span)
            tiles = total_ref[rows, :].astype(BF16)
            if role in (2, 3, 5):
                tiles = dot_nn(tiles, swap_ref[...]).astype(BF16)
            out_ref[rows, :] = tiles


def select_tiles(row_of, swap, received):
    depth, lanes = received.shape
    chunk = math.gcd(depth, 1024) if depth % 1024 == 0 else math.gcd(depth, 512)
    wanted = row_of.shape[0]
    return pl.pallas_call(
        select_body,
        grid=(depth // chunk,),
        in_specs=[
            pl.BlockSpec((wanted, 1), lambda k: (0, 0)),
            pl.BlockSpec((lanes, lanes), lambda k: (0, 0)),
            pl.BlockSpec((chunk, lanes), lambda k: (k, 0)),
        ],
        out_specs=pl.BlockSpec((wanted, lanes), lambda k: (0, 0)),
        out_shape=jax.ShapeDtypeStruct((wanted, lanes), BF16),
        scratch_shapes=[pltpu.VMEM((wanted, lanes), F32)],
        compiler_params=params(),
        name="select_tiles",
    )(row_of.reshape(wanted, 1), swap, received)


def exchange(read_lanes, trade, write, width):
    lanes = width * width
    blocks = lanes // 128
    low = 128 // width
    high = width // low
    for block in range(blocks):
        piece = read_lanes(block).reshape(high, low, width, 128)
        wide = jnp.concatenate(
            [piece[:, part].reshape(high * width, 128) for part in range(low)], axis=1
        )
        traded = dot_nn(wide, trade).astype(BF16)
        for part in range(low):
            group = traded[:, part * 128 : (part + 1) * 128].reshape(high, width, 128)
            for lead in range(high):
                write(block * low + part, lead, group[lead])


def regroup_body(swap_ref, trade_ref, block_ref, first_ref, second_ref, swapped_ref, *, width):
    lanes = width * width
    half = lanes // 2
    for part in range(2):
        span = slice(part * half, (part + 1) * half)
        swapped_ref[:, span] = dot_nn(block_ref[0], swap_ref[:, span]).astype(BF16)

    def writer(out_ref):
        def write(row_block, lane_block, value):
            out_ref[
                0,
                row_block * width : (row_block + 1) * width,
                lane_block * 128 : (lane_block + 1) * 128,
            ] = value

        return write

    exchange(
        lambda b: swapped_ref[:, b * 128 : (b + 1) * 128],
        trade_ref[...],
        writer(first_ref),
        width,
    )
    exchange(
        lambda b: block_ref[0, :, b * 128 : (b + 1) * 128],
        trade_ref[...],
        writer(second_ref),
        width,
    )


def regroup(integrals, swap, trade):
    count, lanes, _ = integrals.shape
    width = math.isqrt(lanes)
    whole = pl.BlockSpec((1, lanes, lanes), lambda i: (i, 0, 0))
    out = jax.ShapeDtypeStruct(integrals.shape, BF16)
    return pl.pallas_call(
        functools.partial(regroup_body, width=width),
        grid=(count,),
        in_specs=[
            pl.BlockSpec(swap.shape, lambda i: (0, 0)),
            pl.BlockSpec(trade.shape, lambda i: (0, 0)),
            whole,
        ],
        out_specs=[whole, whole],
        out_shape=[out, out],
        scratch_shapes=[pltpu.VMEM((lanes, lanes), BF16)],
        compiler_params=params(),
        cost_estimate=cost(count * 4 * lanes**3, count * 6 * lanes**2),
        name="regroup",
    )(swap, trade, integrals)


def contract_body(tiles_ref, block_ref, first_ref, second_ref, high_ref, low_ref):
    block, first, second = block_ref[0], first_ref[0], second_ref[0]

    def tile(role):
        return tiles_ref[role, 0]

    def put(role, term):
        top = term.astype(BF16)
        high_ref[role, 0] = top
        low_ref[role, 0] = (term - top.astype(F32)).astype(BF16)

    put(0, 2.0 * dot_nt(tile(4), block))
    put(4, 2.0 * dot_nn(tile(0), block))
    put(1, -dot_nn(tile(3), first))
    put(3, -dot_nt(tile(1), first))
    put(2, -dot_nt(tile(5), second))
    put(5, -dot_nn(tile(2), second))


def contract(tiles, integrals, first, second):
    count, lanes, _ = integrals.shape
    whole = pl.BlockSpec((1, lanes, lanes), lambda i: (i, 0, 0))
    part = pl.BlockSpec((ROLES, 1, PAD_N, lanes), lambda i: (0, i, 0, 0))
    out = jax.ShapeDtypeStruct((ROLES, count, PAD_N, lanes), BF16)
    return pl.pallas_call(
        contract_body,
        grid=(count,),
        in_specs=[part, whole, whole, whole],
        out_specs=[part, part],
        out_shape=[out, out],
        compiler_params=params(),
        name="contract",
    )(tiles, integrals, first, second)


def pack_body(target_ref, swap_ref, high_ref, low_ref, out_ref, terms_ref):
    half = high_ref.shape[0]

    @pl.when(pl.program_id(0) == 0)
    def _():
        span = half // ROLES
        for which, source in enumerate((high_ref, low_ref)):
            for role in range(ROLES):
                rows = source[role * span : (role + 1) * span, :]
                if role in (2, 3, 5):
                    rows = dot_nn(rows, swap_ref[...]).astype(BF16)
                start = which * half + role * span
                terms_ref[start : start + span, :] = rows

    out_ref[...] = dot_nn(hot_rows(target_ref[...], 2 * half), terms_ref[...]).astype(BF16)


def pack_terms(row_of, swap, high, low):
    count = row_of.shape[0]
    half, lanes = high.shape
    chunk = math.gcd(count, 512)
    return pl.pallas_call(
        pack_body,
        grid=(count // chunk,),
        in_specs=[
            pl.BlockSpec((chunk, 1), lambda k: (k, 0)),
            pl.BlockSpec((lanes, lanes), lambda k: (0, 0)),
            pl.BlockSpec((half, lanes), lambda k: (0, 0)),
            pl.BlockSpec((half, lanes), lambda k: (0, 0)),
        ],
        out_specs=pl.BlockSpec((chunk, lanes), lambda k: (k, 0)),
        out_shape=jax.ShapeDtypeStruct((count, lanes), BF16),
        scratch_shapes=[pltpu.VMEM((2 * half, lanes), BF16)],
        compiler_params=params(),
        name="pack_terms",
    )(row_of.reshape(count, 1), swap, high, low)


def scatter_body(target_ref, slots_ref, out_ref, hot_ref):
    rows_dev, per, blocks, lanes = out_ref.shape
    height = per * blocks
    depth = hot_ref.shape[1]

    @pl.when(pl.program_id(0) == 0)
    def _():
        hot_ref[...] = hot_columns(target_ref[...], rows_dev * height)

    slots = slots_ref[...].reshape(depth, lanes)
    for row in range(rows_dev):
        total = dot_nn(hot_ref[row * height : (row + 1) * height, :], slots)
        out_ref[row] = total.astype(BF16).reshape(per, blocks, lanes)


def scatter_terms(landing, arrived, rows_dev, blocks):
    peers, slots = landing.shape
    _, groups, _, lanes = arrived.shape
    per = ROWS // slots
    inner = jnp.arange(per, dtype=jnp.int32)[None, :, None]
    target = (landing // blocks)[:, None, :] * (per * blocks) + inner * blocks
    target = target + (landing % blocks)[:, None, :]
    target = jnp.where(landing[:, None, :] >= 0, target, -1).reshape(1, peers * ROWS)
    return pl.pallas_call(
        scatter_body,
        grid=(groups,),
        in_specs=[
            pl.BlockSpec((1, peers * ROWS), lambda g: (0, 0)),
            pl.BlockSpec((peers, 1, ROWS, lanes), lambda g: (0, g, 0, 0)),
        ],
        out_specs=pl.BlockSpec((rows_dev, per, blocks, lanes), lambda g: (0, g, 0, 0)),
        out_shape=jax.ShapeDtypeStruct((rows_dev, groups * per, blocks, lanes), BF16),
        scratch_shapes=[pltpu.VMEM((rows_dev * per * blocks, peers * ROWS), BF16)],
        compiler_params=params(),
        name="scatter_terms",
    )(target, arrived)


def tile_slots(quartets, owner_map, rows_dev):
    blocks_total = owner_map.shape[0]
    lead_shape = quartets.shape[:-2]
    row_blocks = jnp.stack([quartets[..., pick] for pick in ROLE_ROW], -2)
    col_blocks = jnp.stack([quartets[..., pick] for pick in ROLE_COL], -2)
    row_blocks = row_blocks.reshape(lead_shape + (-1,))
    col_blocks = col_blocks.reshape(lead_shape + (-1,))
    block_ids = jnp.arange(blocks_total, dtype=jnp.int32)
    storage = jnp.sum(jnp.where(row_blocks[..., None] == block_ids, owner_map, 0), axis=-1)
    target = storage // rows_dev
    local_tile = storage % rows_dev * blocks_total + col_blocks
    positions = jnp.arange(target.shape[-1])
    earlier = (target[..., None, :] == target[..., :, None]) & (
        positions[None, :] < positions[:, None]
    )
    slot_rank = jnp.sum(earlier.astype(jnp.int32), axis=-1)
    return target, slot_rank, local_tile


def permutation_tables(width):
    lanes = width * width
    low = 128 // width
    index = jnp.arange(lanes, dtype=jnp.int32)
    partner = index % width * width + index // width
    swap = (index[:, None] == partner[None, :]).astype(BF16)
    span = jnp.arange(low * 128, dtype=jnp.int32)
    lead, group, inner = span // 128, span % 128 // width, span % width
    partner = group * 128 + lead * width + inner
    trade = (span[None, :] == partner[:, None]).astype(BF16)
    return swap, trade


def slot_count(most):
    for slots in (4, 8, 16):
        if most <= slots:
            return slots
    raise ValueError(most)


def exchange_slots(array):
    return lax.all_to_all(array, AXES, split_axis=0, concat_axis=0, tiled=True)


def local(integrals, quartets, density, owner_map):
    rows_dev, blocks_total, dens_count, tile_len = density.shape
    devices = lax.axis_size(AXES)
    quartet_count = quartets.shape[0]
    tile_count = ROLES * quartet_count
    width = math.isqrt(tile_len)
    peer_most = 2 * rows_dev
    slots = slot_count(peer_most)
    per = ROWS // slots
    target, slot_rank, local_tile = tile_slots(quartets, owner_map, rows_dev)
    slot_index = target * slots + slot_rank
    slot_hit = slot_index[None, :] == jnp.arange(devices * slots)[:, None]
    requests = jnp.sum(jnp.where(slot_hit, local_tile[None, :] + 1, 0), axis=1) - 1
    tile_ids = jnp.arange(tile_count, dtype=jnp.int32)
    tile_of_slot = jnp.sum(jnp.where(slot_hit, tile_ids[None, :] + 1, 0), axis=1) - 1
    incoming = exchange_slots(requests.reshape(devices, slots))

    swap, trade = permutation_tables(width)
    density_rows = jnp.transpose(density, (0, 2, 1, 3))
    sent = gather_tiles(incoming, density_rows, slots)
    returned = exchange_slots(sent)
    first, second = regroup(integrals, swap, trade)

    dens_ids = jnp.arange(PAD_N, dtype=jnp.int32)[None, :]
    row_of = (
        target[:, None] * (dens_count * slots)
        + dens_ids // per * ROWS
        + dens_ids % per * slots
        + slot_rank[:, None]
    )
    row_of = jnp.where(dens_ids < dens_count, row_of, -1).reshape(-1)
    tiles = select_tiles(row_of, swap, returned.reshape(-1, tile_len))
    tiles = tiles.reshape(ROLES, quartet_count, PAD_N, tile_len)
    high, low = contract(tiles, integrals, first, second)

    out_slots = slot_count(2 * slots)
    out_per = ROWS // out_slots
    shape = (devices, dens_count // out_per, out_per, out_slots)
    tile_of_slot = tile_of_slot.reshape(devices, slots)
    none = jnp.full((devices, out_slots // 2 - slots), -1, jnp.int32)
    low_tile = jnp.where(tile_of_slot >= 0, tile_of_slot + tile_count, -1)
    term_of_slot = jnp.concatenate([tile_of_slot, none, low_tile, none], axis=1)
    dens_of = jnp.arange(dens_count, dtype=jnp.int32).reshape(1, shape[1], out_per, 1)
    term_row = term_of_slot[:, None, None, :] * PAD_N + dens_of
    term_row = jnp.where(term_of_slot[:, None, None, :] >= 0, term_row, -1)
    outgoing = pack_terms(
        term_row.reshape(-1),
        swap,
        high.reshape(tile_count * PAD_N, tile_len),
        low.reshape(tile_count * PAD_N, tile_len),
    )
    arrived = exchange_slots(outgoing.reshape(devices, shape[1], ROWS, tile_len))
    landing = jnp.concatenate([incoming, none, incoming, none], axis=1)
    fock = scatter_terms(landing, arrived, rows_dev, blocks_total)
    return jnp.transpose(fock, (0, 2, 1, 3))


def solution(mesh):
    return jax.shard_map(
        local,
        mesh=mesh,
        in_specs=(
            P(AXES, None, None),
            P(AXES, None),
            P(AXES, None, None, None),
            P(),
        ),
        out_specs=P(AXES, None, None, None),
        check_vma=False,
    )
```

time: 1020 us -> 537 us (0.53); the launches traced: 998 us -> 537 us
  local copies, waits for them, and re-layouts: 578 us -> 7.47 us
  Pallas kernels: 0 us -> 133 us
  waiting for transfers between devices: 277 us -> 376 us
  other arithmetic: 68.5 us -> 5.48 us
  matrix products: 54.3 us -> 0 us
    reshape x8 -> x1, local copies, waits for them, and re-layouts: 326 us -> 0.08 us  [tile_slots(): col_blocks = col_blocks.reshape(lead_shape + (-1,))]
    transpose x2 -> x0, local copies, waits for them, and re-layouts: 143 us -> none  [the longest x1 98.3 us: contract_all(): jnp.transpose(split_blocks, (0, 2, 3, 4, 1))]
    pallas_call x0 -> x6, Pallas kernels: none -> 133 us  [the longest x1 41.1 us: regroup(): pl.pallas_call(functools.partial(regroup_body, width=width), grid=(count,...]
    all_to_all x3, waiting for transfers between devices: 277 us -> 376 us  [exchange_slots(): return lax.all_to_all(array, AXES, split_axis=0, concat_axis=0, tiled=True)]
    scatter-add x1 -> x0, other arithmetic: 57 us -> none  [local(): fock_rows = jnp.zeros((rows_dev * blocks_total, dens_count, tile_len), jn...]
    dot_general x6 -> x0, matrix products: 54.3 us -> none  [the longest x1 11.2 us: contract_all(): jnp.einsum('iab,inb->ina', pr_layout, read_tiles[:, 3], preferred_element...]
    all_to_all x5 -> x1, local copies, waits for them, and re-layouts: 24.4 us -> 0.06 us  [exchange_slots(): return lax.all_to_all(array, AXES, split_axis=0, concat_axis=0, tiled=True)]
    scatter-add x1 -> x0, local copies, waits for them, and re-layouts: 24.3 us -> none  [local(): fock_rows = jnp.zeros((rows_dev * blocks_total, dens_count, tile_len), jn...]
  transfers between devices with their start and end apart: 3 -> 3, of which waited for: 1 -> 3; matrix products, arithmetic and copies ran while one was open for 43% -> 2% of each run, Pallas kernels for 0% -> 8%
where the time goes in v1:
time: 537 us
  waiting for transfers between devices  376 us (70%)
  Pallas kernels  133 us (25%)
  starting transfers between devices  14.7 us (3%)
  local copies, waits for them, and re-layouts  7.47 us (1%)
  other arithmetic  5.48 us (1%)
    all_to_all x3, waiting for transfers between devices, exchange_slots(): return lax.all_to_all(array, AXES, split_axis=0, concat_axis=0, tiled=True)  376 us
    pallas_call x1, Pallas kernels, regroup(): pl.pallas_call(functools.partial(regroup_body, width=width), grid=(count,...  41.1 us
    pallas_call x1, Pallas kernels, pack_terms(): pl.pallas_call(pack_body, grid=(count // chunk,), in_specs=[pl.BlockSpec(...  27.8 us
    pallas_call x1, Pallas kernels, contract(): pl.pallas_call(contract_body, grid=(count,), in_specs=[part, whole, whole...  26 us
    pallas_call x1, Pallas kernels, scatter_terms(): pl.pallas_call(scatter_body, grid=(groups,), in_specs=[pl.BlockSpec((1, p...  15.9 us
    all_to_all x3, starting transfers between devices, exchange_slots(): return lax.all_to_all(array, AXES, split_axis=0, concat_axis=0, tiled=True)  14.7 us
    pallas_call x1, Pallas kernels, gather_tiles(): pl.pallas_call(gather_body, grid=(groups,), in_specs=[pl.BlockSpec((peers...  12.1 us
  transfers between devices with their start and end apart: 3, of which 3 were waited for; matrix products, arithmetic and copies ran while one was open for 2% of the time, Pallas kernels for 8%

profile of v1, /device:TPU:0, one launch (start us, length us, event | category | flops | bytes accessed | tf_op | source)
XLA Modules:
  0.0 536.6 jit_solution(11156779098775063892)
XLA Ops:
  0.0 0.8 slice_bitcast_fusion
  1.0 0.8 select_reduce_fusion.2
  1.9 0.2 convert_reduce_fusion
  2.1 0.1 select_reduce_fusion
  2.2 0.7 sub.54
  2.9 7.3 %all-to-all-start = ((s32[32,1,8]{2,1,0:T(1,128)}), s32[32,1,8]{2,1,0:T(1,128)S(1)}, u32[]{:S(2)}, u32[]{:S(2)}) async-start(s32[32,1,8]{2,1,0:T(1,128)} %bitcast.4), calls=%async_computation | async-start | bytes 32768 | tf_op jit(solution)/shard_map/all_to_all | solution.py:353
  10.3 7.1 %all-to-all-done = s32[32,1,8]{2,1,0:T(1,128)S(1)} async-done(((s32[32,1,8]{2,1,0:T(1,128)}), s32[32,1,8]{2,1,0:T(1,128)S(1)}, u32[]{:S(2)}, u32[]{:S(2)}) %all-to-all-start) | async-done | bytes 1056 | tf_op jit(solution)/shard_map/all_to_all | solution.py:353
  17.8 0.8 select_n.254.target_ref
  18.6 12.1 %gather_tiles.1 = bf16[32,6,16,1024]{3,2,1,0:T(8,128)(2,1)} custom-call(s32[512,1]{1,0:T(8,128)} %select_n.254.target_ref, bf16[4,12,128,1024]{3,2,1,0:T(8,128)(2,1)} %bitcast.25), custom_call_target="tpu_custom_call" | custom-call | tf_op jit(solution)/shard_map/gather_tiles/pallas_call | solution.py:76
  30.8 3.6 all-to-all-start.1
  34.5 1.0 select_n.253.target_ref
  35.9 3.4 select_n.252.target_ref
  39.2 0.9 fusion.1.trade_ref
  40.2 2.2 fusion.swap_ref
  42.4 41.1 %regroup.1 = (bf16[8,1024,1024]{2,1,0:T(8,128)(2,1)}, bf16[8,1024,1024]{2,1,0:T(8,128)(2,1)}) custom-call(bf16[1024,1024]{1,0:T(8,128)(2,1)} %fusion.swap_ref, bf16[512,512]{1,0:T(8,128)(2,1)} %fusion.1.trade_ref, bf16[8,1024,1024]{2,1,0:T(8,128)(2,1)} %block_ref.3), custom_call_target="tpu_custom_call" | custom-call | flops 34359738368 | bytes 50331648 | tf_op jit(solution)/shard_map/regroup/pallas_call | solution.py:185
  83.5 90.6 %all-to-all-done.1 = bf16[32,6,16,1024]{3,2,1,0:T(8,128)(2,1)} async-done(((bf16[32,6,16,1024]{3,2,1,0:T(8,128)(2,1)}), bf16[32,6,16,1024]{3,2,1,0:T(8,128)(2,1)}, u32[]{:S(2)}, u32[]{:S(2)}) %all-to-all-start.1) | async-done | bytes 6291488 | tf_op jit(solution)/shard_map/all_to_all | solution.py:353
  174.1 10.3 %select_tiles.1 = bf16[768,1024]{1,0:T(8,128)(2,1)} custom-call(s32[768,1]{1,0:T(8,128)} %select_n.253.target_ref, bf16[1024,1024]{1,0:T(8,128)(2,1)} %fusion.swap_ref, bf16[3072,1024]{1,0:T(8,128)(2,1)} %bitcast.9.slots_ref), custom_call_target="tpu_custom_call" | custom-call | tf_op jit(solution)/shard_map/select_tiles/pallas_call | solution.py:116
  184.4 26.0 %contract.1 = (bf16[6,8,16,1024]{3,2,1,0:T(8,128)(2,1)}, bf16[6,8,16,1024]{3,2,1,0:T(8,128)(2,1)}) custom-call(bf16[6,8,16,1024]{3,2,1,0:T(8,128)(2,1)} %bitcast.26, bf16[8,1024,1024]{2,1,0:T(8,128)(2,1)} %block_ref.3, bf16[8,1024,1024]{2,1,0:T(8,128)(2,1)} %get-tuple-element.9.first_ref, bf16[8,1024,1024]{2,1,0:T(8,128)(2,1)} %get-tuple-element.10.second_ref), custom_call_target="tpu_custom_call" | custom-call | tf_op jit(solution)/shard_map/contract/pallas_call | solution.py:226
  210.4 27.8 %pack_terms.1 = bf16[6144,1024]{1,0:T(8,128)(2,1)} custom-call(s32[6144,1]{1,0:T(8,128)} %select_n.252.target_ref, bf16[1024,1024]{1,0:T(8,128)(2,1)} %fusion.swap_ref, bf16[768,1024]{1,0:T(8,128)(2,1)} %bitcast.27, bf16[768,1024]{1,0:T(8,128)(2,1)} %bitcast.28), custom_call_target="tpu_custom_call" | custom-call | tf_op jit(solution)/shard_map/pack_terms/pallas_call | solution.py:258
  238.2 3.8 all-to-all-start.2
  242.0 0.1 add_reduce_fusion
  242.2 0.6 compare_select_fusion.1.target_ref
  242.8 277.8 %all-to-all-done.2.slots_ref = bf16[32,12,16,1024]{3,2,1,0:T(8,128)(2,1)} async-done(((bf16[32,12,16,1024]{3,2,1,0:T(8,128)(2,1)}), bf16[32,12,16,1024]{3,2,1,0:T(8,128)(2,1)}, u32[]{:S(2)}, u32[]{:S(2)}) %all-to-all-start.2) | async-done | bytes 12582944 | tf_op jit(solution)/shard_map/all_to_all | solution.py:353
  520.6 15.9 %scatter_terms.1 = bf16[4,12,128,1024]{3,2,1,0:T(8,128)(2,1)} custom-call(s32[1,512]{1,0:T(1,128)} %compare_select_fusion.1.target_ref, bf16[32,12,16,1024]{3,2,1,0:T(8,128)(2,1)} %all-to-all-done.2.slots_ref), custom_call_target="tpu_custom_call" | custom-call | tf_op jit(solution)/shard_map/scatter_terms/pallas_call | solution.py:298
  (28 shorter events, 1.2 us)
Async XLA Ops:
  2.9 14.4 %all-to-all-start = ((s32[32,1,8]{2,1,0:T(1,128)}), s32[32,1,8]{2,1,0:T(1,128)S(1)}, u32[]{:S(2)}, u32[]{:S(2)}) async-start(s32[32,1,8]{2,1,0:T(1,128)} %bitcast.4), calls=%async_computation | async-start | bytes 32768 | tf_op jit(solution)/shard_map/all_to_all | solution.py:353
  30.8 143.4 %all-to-all-start.1 = ((bf16[32,6,16,1024]{3,2,1,0:T(8,128)(2,1)}), bf16[32,6,16,1024]{3,2,1,0:T(8,128)(2,1)}, u32[]{:S(2)}, u32[]{:S(2)}) async-start(bf16[32,6,16,1024]{3,2,1,0:T(8,128)(2,1)} %gather_tiles.1), calls=%async_computation.1 | async-start | bytes 12582912 | tf_op jit(solution)/shard_map/all_to_all | solution.py:353
  238.2 282.4 %all-to-all-start.2 = ((bf16[32,12,16,1024]{3,2,1,0:T(8,128)(2,1)}), bf16[32,12,16,1024]{3,2,1,0:T(8,128)(2,1)}, u32[]{:S(2)}, u32[]{:S(2)}) async-start(bf16[32,12,16,1024]{3,2,1,0:T(8,128)(2,1)} %bitcast.24), calls=%async_computation.2 | async-start | bytes 25165824 | tf_op jit(solution)/shard_map/all_to_all | solution.py:353

commit v2 on v1

--- a/solution.py
+++ b/solution.py
@@ -17,6 +17,10 @@
 BF16 = jnp.bfloat16
 F32 = jnp.float32
 VMEM_BYTES = 60 * 1024 * 1024
+FIRST_SLOTS = 4
+RELAY_ROWS = 4
+READ_SPARE = 8
+TERM_SPARE = 16
 
 
 def params(axes=1):
@@ -45,6 +49,31 @@
 
 def dot_nt(left, right):
     return lax.dot_general(left, right, (((1,), (1,)), ((), ())), preferred_element_type=F32)
+
+
+def tile_rows(tiles, per, blocks):
+    inner = jnp.arange(per, dtype=jnp.int32)[None, :, None]
+    rows = (tiles // blocks * (per * blocks) + tiles % blocks)[:, None, :] + inner * blocks
+    return jnp.where(tiles[:, None, :] >= 0, rows, -1)
+
+
+def slot_rows(slot, slots, dens):
+    per = ROWS // slots
+    ids = jnp.arange(dens, dtype=jnp.int32)
+    rows = (slot // slots * (dens * slots) + slot % slots)[..., None]
+    rows = rows + ids // per * ROWS + ids % per * slots
+    return jnp.where(slot[..., None] >= 0, rows, -1)
+
+
+def relay_rows(peer, peers, dens):
+    ids = jnp.arange(dens, dtype=jnp.int32)
+    rows = peer[..., None] * RELAY_ROWS + ids // RELAY_ROWS * (peers * RELAY_ROWS) + ids % RELAY_ROWS
+    return jnp.where(peer[..., None] >= 0, rows, -1)
+
+
+def pad_rows(rows):
+    pad = [(0, 0)] * (rows.ndim - 1) + [(0, PAD_N - rows.shape[-1])]
+    return jnp.pad(rows, pad, constant_values=-1).reshape(-1)
 
 
 def gather_body(target_ref, density_ref, out_ref, hot_ref):
@@ -69,10 +98,7 @@
     per = ROWS // slots
     groups = dens // per
     depth = rows_dev * per * blocks
-    tile_row, tile_col = wanted // blocks, wanted % blocks
-    inner = jnp.arange(per, dtype=jnp.int32)[None, :, None]
-    target = tile_row[:, None, :] * (per * blocks) + inner * blocks + tile_col[:, None, :]
-    target = jnp.where(wanted[:, None, :] >= 0, target, -1).reshape(peers * ROWS, 1)
+    target = tile_rows(wanted, per, blocks).reshape(peers * ROWS, 1)
     return pl.pallas_call(
         gather_body,
         grid=(groups,),
@@ -88,18 +114,30 @@
     )(target, density_rows)
 
 
-def select_body(target_ref, swap_ref, slots_ref, out_ref, total_ref):
+def pick_body(*refs, relay, swapped):
+    if relay:
+        relay_target_ref, relayed_ref, *refs = refs
+    if swapped:
+        swap_ref, *refs = refs
+    target_ref, slots_ref, out_ref, total_ref = refs
     step = pl.program_id(0)
-    depth, lanes = slots_ref.shape
+    depth = slots_ref.shape[0]
 
     @pl.when(step == 0)
     def _():
-        total_ref[...] = jnp.zeros_like(total_ref)
+        if relay:
+            hot = hot_rows(relay_target_ref[...], relayed_ref.shape[0])
+            total_ref[...] = dot_nn(hot, relayed_ref[...])
+        else:
+            total_ref[...] = jnp.zeros_like(total_ref)
 
     total_ref[...] += dot_nn(hot_rows(target_ref[...], depth, step * depth), slots_ref[...])
 
     @pl.when(step == pl.num_programs(0) - 1)
     def _():
+        if not swapped:
+            out_ref[...] = total_ref[...].astype(BF16)
+            return
         span = out_ref.shape[0] // ROLES
         for role in range(ROLES):
             rows = slice(role * span, (role + 1) * span)
@@ -109,24 +147,28 @@
             out_ref[rows, :] = tiles
 
 
-def select_tiles(row_of, swap, received):
+def pick_rows(row_of, received, swap=None, relay_row_of=None, relayed=None):
     depth, lanes = received.shape
     chunk = math.gcd(depth, 1024) if depth % 1024 == 0 else math.gcd(depth, 512)
     wanted = row_of.shape[0]
+    column = pl.BlockSpec((wanted, 1), lambda k: (0, 0))
+    specs, operands = [], []
+    if relayed is not None:
+        specs += [column, pl.BlockSpec(relayed.shape, lambda k: (0, 0))]
+        operands += [relay_row_of.reshape(wanted, 1), relayed]
+    if swap is not None:
+        specs += [pl.BlockSpec(swap.shape, lambda k: (0, 0))]
+        operands += [swap]
     return pl.pallas_call(
-        select_body,
+        functools.partial(pick_body, relay=relayed is not None, swapped=swap is not None),
         grid=(depth // chunk,),
-        in_specs=[
-            pl.BlockSpec((wanted, 1), lambda k: (0, 0)),
-            pl.BlockSpec((lanes, lanes), lambda k: (0, 0)),
-            pl.BlockSpec((chunk, lanes), lambda k: (k, 0)),
-        ],
+        in_specs=[*specs, column, pl.BlockSpec((chunk, lanes), lambda k: (k, 0))],
         out_specs=pl.BlockSpec((wanted, lanes), lambda k: (0, 0)),
         out_shape=jax.ShapeDtypeStruct((wanted, lanes), BF16),
         scratch_shapes=[pltpu.VMEM((wanted, lanes), F32)],
         compiler_params=params(),
-        name="select_tiles",
-    )(row_of.reshape(wanted, 1), swap, received)
+        name="pick_rows",
+    )(*operands, row_of.reshape(wanted, 1), received)
 
 
 def exchange(read_lanes, trade, write, width):
@@ -272,7 +314,10 @@
     )(row_of.reshape(count, 1), swap, high, low)
 
 
-def scatter_body(target_ref, slots_ref, out_ref, hot_ref):
+def scatter_body(*refs, relay):
+    if relay:
+        relay_target_ref, relayed_ref, *refs, relay_hot_ref = refs
+    target_ref, slots_ref, out_ref, hot_ref = refs
     rows_dev, per, blocks, lanes = out_ref.shape
     height = per * blocks
     depth = hot_ref.shape[1]
@@ -280,53 +325,133 @@
     @pl.when(pl.program_id(0) == 0)
     def _():
         hot_ref[...] = hot_columns(target_ref[...], rows_dev * height)
+        if relay:
+            relay_hot_ref[...] = hot_columns(relay_target_ref[...], rows_dev * height)
 
     slots = slots_ref[...].reshape(depth, lanes)
     for row in range(rows_dev):
-        total = dot_nn(hot_ref[row * height : (row + 1) * height, :], slots)
+        span = slice(row * height, (row + 1) * height)
+        total = dot_nn(hot_ref[span, :], slots)
+        if relay:
+            total += dot_nn(relay_hot_ref[span, :], relayed_ref[0])
         out_ref[row] = total.astype(BF16).reshape(per, blocks, lanes)
 
 
-def scatter_terms(landing, arrived, rows_dev, blocks):
+def scatter_terms(landing, arrived, rows_dev, blocks, relay_landing=None, relayed=None):
     peers, slots = landing.shape
     _, groups, _, lanes = arrived.shape
     per = ROWS // slots
-    inner = jnp.arange(per, dtype=jnp.int32)[None, :, None]
-    target = (landing // blocks)[:, None, :] * (per * blocks) + inner * blocks
-    target = target + (landing % blocks)[:, None, :]
-    target = jnp.where(landing[:, None, :] >= 0, target, -1).reshape(1, peers * ROWS)
+    high = rows_dev * per * blocks
+    specs, operands = [], []
+    scratch = [pltpu.VMEM((high, peers * ROWS), BF16)]
+    if relayed is not None:
+        depth = relayed.shape[1]
+        specs = [
+            pl.BlockSpec((1, depth), lambda g: (0, 0)),
+            pl.BlockSpec((1, depth, lanes), lambda g: (g, 0, 0)),
+        ]
+        operands = [tile_rows(relay_landing[:, None], per, blocks).reshape(1, depth), relayed]
+        scratch += [pltpu.VMEM((high, depth), BF16)]
     return pl.pallas_call(
-        scatter_body,
+        functools.partial(scatter_body, relay=relayed is not None),
         grid=(groups,),
         in_specs=[
+            *specs,
             pl.BlockSpec((1, peers * ROWS), lambda g: (0, 0)),
             pl.BlockSpec((peers, 1, ROWS, lanes), lambda g: (0, g, 0, 0)),
         ],
         out_specs=pl.BlockSpec((rows_dev, per, blocks, lanes), lambda g: (0, g, 0, 0)),
         out_shape=jax.ShapeDtypeStruct((rows_dev, groups * per, blocks, lanes), BF16),
-        scratch_shapes=[pltpu.VMEM((rows_dev * per * blocks, peers * ROWS), BF16)],
+        scratch_shapes=scratch,
         compiler_params=params(),
         name="scatter_terms",
-    )(target, arrived)
-
-
-def tile_slots(quartets, owner_map, rows_dev):
-    blocks_total = owner_map.shape[0]
-    lead_shape = quartets.shape[:-2]
-    row_blocks = jnp.stack([quartets[..., pick] for pick in ROLE_ROW], -2)
-    col_blocks = jnp.stack([quartets[..., pick] for pick in ROLE_COL], -2)
-    row_blocks = row_blocks.reshape(lead_shape + (-1,))
-    col_blocks = col_blocks.reshape(lead_shape + (-1,))
-    block_ids = jnp.arange(blocks_total, dtype=jnp.int32)
-    storage = jnp.sum(jnp.where(row_blocks[..., None] == block_ids, owner_map, 0), axis=-1)
-    target = storage // rows_dev
-    local_tile = storage % rows_dev * blocks_total + col_blocks
-    positions = jnp.arange(target.shape[-1])
-    earlier = (target[..., None, :] == target[..., :, None]) & (
-        positions[None, :] < positions[:, None]
-    )
-    slot_rank = jnp.sum(earlier.astype(jnp.int32), axis=-1)
-    return target, slot_rank, local_tile
+    )(*operands, tile_rows(landing, per, blocks).reshape(1, peers * ROWS), arrived)
+
+
+def route_body(list_ref, state_hbm, out_ref, state_ref, sem, *, peers, spare, scale, outward):
+    copy = pltpu.make_async_copy(state_hbm, state_ref, sem)
+    copy.start()
+    copy.wait()
+    used_at = peers * peers
+
+    def count_at(source, middle):
+        return source * peers + middle if outward else middle * peers + source
+
+    def one(index, failed):
+        value = list_ref[index]
+        row = index // spare
+        other = jnp.maximum(value, 0) // scale
+        source, last = (row, other) if outward else (other, row)
+
+        def search(carry):
+            tries, middle, found = carry
+            full = state_ref[count_at(source, middle)] >= FIRST_SLOTS
+            taken = state_ref[used_at + middle * peers + last] > 0
+            found = jnp.where(full | taken, found, middle)
+            following = jnp.where(middle + 1 == peers, 0, middle + 1)
+            return tries + 1, following, found
+
+        start = source + last
+        start = jnp.where(start >= peers, start - peers, start)
+        tries = jnp.where(value >= 0, 0, peers)
+        _, _, found = lax.while_loop(
+            lambda carry: (carry[0] < peers) & (carry[2] < 0), search, (tries, start, jnp.int32(-1))
+        )
+        out_ref[index] = -1
+
+        @pl.when(found >= 0)
+        def _():
+            place = count_at(source, found)
+            count = state_ref[place]
+            out_ref[index] = found * FIRST_SLOTS + count
+            state_ref[place] = count + 1
+            state_ref[used_at + found * peers + last] = 1
+
+        return failed + jnp.where((value >= 0) & (found < 0), 1, 0)
+
+    out_ref[peers * spare] = lax.fori_loop(0, peers * spare, one, jnp.int32(0))
+
+
+def route(lists, counts, scale, outward):
+    peers, spare = lists.shape
+    state = jnp.concatenate([counts, jnp.zeros_like(counts)]).reshape(-1)
+    smem = pl.BlockSpec(memory_space=pltpu.SMEM)
+    out = pl.pallas_call(
+        functools.partial(
+            route_body, peers=peers, spare=spare, scale=scale, outward=outward
+        ),
+        in_specs=[smem, pl.BlockSpec(memory_space=pl.ANY)],
+        out_specs=smem,
+        out_shape=jax.ShapeDtypeStruct((peers * spare + 1,), jnp.int32),
+        scratch_shapes=[pltpu.SMEM((2 * peers * peers,), jnp.int32), pltpu.SemaphoreType.DMA],
+        name="route",
+    )(lists.reshape(-1), state)
+    return out[:-1].reshape(peers, spare), out[-1]
+
+
+def tile_keys(quartets, owner_map):
+    blocks = owner_map.shape[0]
+    row_blocks = jnp.stack([quartets[:, pick] for pick in ROLE_ROW]).reshape(-1)
+    col_blocks = jnp.stack([quartets[:, pick] for pick in ROLE_COL]).reshape(-1)
+    ids = jnp.arange(blocks, dtype=jnp.int32)
+    storage = jnp.sum(jnp.where(row_blocks[:, None] == ids, owner_map, 0), axis=-1)
+    return storage * blocks + col_blocks
+
+
+def earlier(flags):
+    ids = jnp.arange(flags.shape[-1])
+    ahead = ids[:, None] < ids[None, :]
+    return jnp.sum((flags[..., :, None] & ahead).astype(jnp.int32), axis=-2)
+
+
+def choose(hit, values, axis):
+    return jnp.sum(jnp.where(hit, values + 1, 0), axis=axis) - 1
+
+
+def spilled(flags, values, spare):
+    place = earlier(flags)
+    hit = flags[..., None] & (place[..., None] == jnp.arange(spare))
+    return choose(hit, values[..., None], -2), jnp.sum(flags.astype(jnp.int32), axis=-1)
 
 
 def permutation_tables(width):
@@ -353,60 +478,180 @@
     return lax.all_to_all(array, AXES, split_axis=0, concat_axis=0, tiled=True)
 
 
+def slot_count(most):
+    for slots in (4, 8, 16):
+        if most <= slots:
+            return slots
+    raise ValueError(most)
+
+
+def exchange_slots(array, axis=0):
+    return lax.all_to_all(array, AXES, split_axis=axis, concat_axis=axis, tiled=True)
+
+
+def relay(slot_of, received, dens):
+    peers = slot_of.shape[0]
+    lanes = received.shape[-1]
+    groups = dens // RELAY_ROWS
+    rows = slot_rows(slot_of, FIRST_SLOTS, dens).reshape(peers, groups, RELAY_ROWS)
+    rows = jnp.transpose(rows, (1, 0, 2)).reshape(-1)
+    sent = pick_rows(rows, received.reshape(-1, lanes))
+    got = exchange_slots(sent.reshape(groups, peers, RELAY_ROWS, lanes), 1)
+    return got.reshape(groups, peers * RELAY_ROWS, lanes)
+
+
 def local(integrals, quartets, density, owner_map):
-    rows_dev, blocks_total, dens_count, tile_len = density.shape
+    rows_dev, blocks, dens, lanes = density.shape
     devices = lax.axis_size(AXES)
+    me = lax.axis_index(AXES)
     quartet_count = quartets.shape[0]
     tile_count = ROLES * quartet_count
-    width = math.isqrt(tile_len)
-    peer_most = 2 * rows_dev
-    slots = slot_count(peer_most)
-    per = ROWS // slots
-    target, slot_rank, local_tile = tile_slots(quartets, owner_map, rows_dev)
-    slot_index = target * slots + slot_rank
-    slot_hit = slot_index[None, :] == jnp.arange(devices * slots)[:, None]
-    requests = jnp.sum(jnp.where(slot_hit, local_tile[None, :] + 1, 0), axis=1) - 1
+    span = rows_dev * blocks
+    most = 2 * rows_dev
+    tag = 1 << (2 * tile_count - 1).bit_length()
+    scale = span * tag
+    device_ids = jnp.arange(devices, dtype=jnp.int32)
     tile_ids = jnp.arange(tile_count, dtype=jnp.int32)
-    tile_of_slot = jnp.sum(jnp.where(slot_hit, tile_ids[None, :] + 1, 0), axis=1) - 1
-    incoming = exchange_slots(requests.reshape(devices, slots))
-
-    swap, trade = permutation_tables(width)
+    place_ids = jnp.arange(FIRST_SLOTS, dtype=jnp.int32)
+
+    key = tile_keys(quartets, owner_map)
+    holder = key // span
+    rank = jnp.sum(
+        ((holder[:, None] == holder) & (tile_ids[:, None] < tile_ids)).astype(jnp.int32), axis=0
+    )
+    asked = jnp.sum((holder[:, None] == device_ids).astype(jnp.int32), axis=0)
+    spare, spare_count = spilled(rank >= FIRST_SLOTS, key * tag + tile_ids, READ_SPARE)
+    message = jnp.concatenate([key * 16 + rank, spare, asked, spare_count[None]])
+    message = jnp.pad(message, (0, -message.shape[0] % 128))
+    told = exchange_slots(jnp.broadcast_to(message, (devices,) + message.shape))
+    keys, ranks = told[:, :tile_count] // 16, told[:, :tile_count] % 16
+    read_list = told[:, tile_count : tile_count + READ_SPARE]
+    counts = told[:, tile_count + READ_SPARE :][:, :devices]
+    spare_counts = told[:, tile_count + READ_SPARE + devices]
+    read_routes, read_misses = route(read_list, counts, scale, False)
+    read_fits = (read_misses == 0) & (jnp.max(spare_counts) <= READ_SPARE)
+
+    homes = keys // span
+    mine = homes == me
+    local_tile = keys - me * span
+    swap, trade = permutation_tables(math.isqrt(lanes))
+
+    def plan_terms():
+        flat = keys.reshape(-1)
+        shared = jnp.sum((flat[:, None] == flat).astype(jnp.int32), axis=0) > 1
+        shared = shared.reshape(keys.shape)
+        ahead = tile_ids[:, None] < tile_ids
+        together = homes[:, :, None] == homes[:, None, :]
+        before = 1 + (shared[:, :, None] & ahead).astype(jnp.int32)
+        low_ranks = jnp.where(shared, jnp.sum(jnp.where(together, before, 0), axis=1), -1)
+        at_home = homes[:, :, None] == device_ids
+        low_counts = jnp.sum((at_home & shared[:, :, None]).astype(jnp.int32), axis=1)
+        both_ranks = jnp.concatenate([ranks, low_ranks], axis=1)
+        values = keys * tag + tile_ids
+        values = jnp.concatenate([values, values + tile_count], axis=1)
+        term_list, term_counts = spilled(both_ranks >= FIRST_SLOTS, values, TERM_SPARE)
+        term_routes, misses = route(term_list, counts + low_counts, scale, True)
+        fits = (misses == 0) & (jnp.max(term_counts) <= TERM_SPARE)
+        return low_ranks, term_list, term_routes, fits
+
+    def requests(slots):
+        hit = mine[:, :, None] & (ranks[:, :, None] == jnp.arange(slots))
+        return choose(hit, local_tile[:, :, None], 1)
+
     density_rows = jnp.transpose(density, (0, 2, 1, 3))
-    sent = gather_tiles(incoming, density_rows, slots)
-    returned = exchange_slots(sent)
-    first, second = regroup(integrals, swap, trade)
-
-    dens_ids = jnp.arange(PAD_N, dtype=jnp.int32)[None, :]
-    row_of = (
-        target[:, None] * (dens_count * slots)
-        + dens_ids // per * ROWS
-        + dens_ids % per * slots
-        + slot_rank[:, None]
-    )
-    row_of = jnp.where(dens_ids < dens_count, row_of, -1).reshape(-1)
-    tiles = select_tiles(row_of, swap, returned.reshape(-1, tile_len))
-    tiles = tiles.reshape(ROLES, quartet_count, PAD_N, tile_len)
-    high, low = contract(tiles, integrals, first, second)
-
-    out_slots = slot_count(2 * slots)
-    out_per = ROWS // out_slots
-    shape = (devices, dens_count // out_per, out_per, out_slots)
-    tile_of_slot = tile_of_slot.reshape(devices, slots)
-    none = jnp.full((devices, out_slots // 2 - slots), -1, jnp.int32)
-    low_tile = jnp.where(tile_of_slot >= 0, tile_of_slot + tile_count, -1)
-    term_of_slot = jnp.concatenate([tile_of_slot, none, low_tile, none], axis=1)
-    dens_of = jnp.arange(dens_count, dtype=jnp.int32).reshape(1, shape[1], out_per, 1)
-    term_row = term_of_slot[:, None, None, :] * PAD_N + dens_of
-    term_row = jnp.where(term_of_slot[:, None, None, :] >= 0, term_row, -1)
-    outgoing = pack_terms(
-        term_row.reshape(-1),
-        swap,
-        high.reshape(tile_count * PAD_N, tile_len),
-        low.reshape(tile_count * PAD_N, tile_len),
-    )
-    arrived = exchange_slots(outgoing.reshape(devices, shape[1], ROWS, tile_len))
-    landing = jnp.concatenate([incoming, none, incoming, none], axis=1)
-    fock = scatter_terms(landing, arrived, rows_dev, blocks_total)
+
+    def read_two_step():
+        list_home = read_list // scale
+        to_send = (read_list >= 0) & (list_home == me)
+        slot_ids = jnp.arange(devices * FIRST_SLOTS, dtype=jnp.int32)
+        hit = to_send.reshape(-1, 1) & (read_routes.reshape(-1, 1) == slot_ids)
+        extra = choose(hit, (read_list // tag - me * span).reshape(-1, 1), 0)
+        wanted = jnp.maximum(requests(FIRST_SLOTS), extra.reshape(devices, FIRST_SLOTS))
+        received = exchange_slots(gather_tiles(wanted, density_rows, FIRST_SLOTS))
+        groups = regroup(integrals, swap, trade)
+        plan = plan_terms()
+        middle, place = read_routes // FIRST_SLOTS, read_routes % FIRST_SLOTS
+        passing = (read_list >= 0) & (middle == me)
+        passed = choose(passing, list_home * FIRST_SLOTS + place, 1)
+        relayed = relay(passed, received, dens)
+        slot = jnp.where(rank < FIRST_SLOTS, holder * FIRST_SLOTS + rank, -1)
+        my_middle = lax.dynamic_index_in_dim(middle, me, 0, keepdims=False)
+        last = (spare[:, None] >= 0) & (spare[:, None] % tag == tile_ids)
+        via = choose(last, my_middle[:, None], 0)
+        tiles = pick_rows(
+            pad_rows(slot_rows(slot, FIRST_SLOTS, dens)),
+            received.reshape(-1, lanes),
+            swap,
+            pad_rows(relay_rows(via, devices, dens)),
+            relayed.reshape(-1, lanes),
+        )
+        return tiles, groups, plan
+
+    def read_one_step():
+        slots = slot_count(most)
+        received = exchange_slots(gather_tiles(requests(slots), density_rows, slots))
+        groups = regroup(integrals, swap, trade)
+        plan = plan_terms()
+        rows = pad_rows(slot_rows(holder * slots + rank, slots, dens))
+        return pick_rows(rows, received.reshape(-1, lanes), swap), groups, plan
+
+    tiles, groups, plan = lax.cond(read_fits, read_two_step, read_one_step)
+    low_ranks, term_list, term_routes, term_fits = plan
+    tiles = tiles.reshape(ROLES, quartet_count, PAD_N, lanes)
+    high, low = contract(tiles, integrals, *groups)
+    high = high.reshape(tile_count * PAD_N, lanes)
+    low = low.reshape(tile_count * PAD_N, lanes)
+
+    def term_rows(term_of_slot, slots):
+        per = ROWS // slots
+        ids = jnp.arange(dens, dtype=jnp.int32).reshape(1, dens // per, per, 1)
+        term = term_of_slot[:, None, None, :]
+        return jnp.where(term >= 0, term * PAD_N + ids, -1).reshape(-1)
+
+    def send(term_of_slot, slots):
+        packed = pack_terms(term_rows(term_of_slot, slots), swap, high, low)
+        return exchange_slots(packed.reshape(devices, dens * slots // ROWS, ROWS, lanes))
+
+    to_holder = holder[:, None] == device_ids
+
+    def write_two_step():
+        my_low = lax.dynamic_index_in_dim(low_ranks, me, 0, keepdims=False)
+        my_list = lax.dynamic_index_in_dim(term_list, me, 0, keepdims=False)
+        my_routes = lax.dynamic_index_in_dim(term_routes, me, 0, keepdims=False)
+        ends = jnp.concatenate([to_holder, to_holder])[:, :, None]
+        places = jnp.concatenate([rank, my_low])[:, None, None] == place_ids
+        both_ids = jnp.arange(2 * tile_count, dtype=jnp.int32)
+        term_of_slot = choose(ends & places, both_ids[:, None, None], 0)
+        slot_ids = jnp.arange(devices * FIRST_SLOTS, dtype=jnp.int32)
+        hit = (my_list[:, None] >= 0) & (my_routes[:, None] == slot_ids)
+        extra = choose(hit, (my_list % tag)[:, None], 0).reshape(devices, FIRST_SLOTS)
+        arrived = send(jnp.maximum(term_of_slot, extra), FIRST_SLOTS)
+        listed = term_list.reshape(-1, 1) >= 0
+        middle = (term_routes // FIRST_SLOTS).reshape(-1, 1)
+        list_home = term_list // scale
+        came = device_ids[:, None] * FIRST_SLOTS + term_routes % FIRST_SLOTS
+        passing = listed & (middle == me) & (list_home.reshape(-1, 1) == device_ids)
+        relayed = relay(choose(passing, came.reshape(-1, 1), 0), arrived, dens)
+        hit = mine[:, :, None] & (ranks[:, :, None] == place_ids)
+        low_hit = mine[:, :, None] & (low_ranks[:, :, None] == place_ids)
+        landing = choose(hit | low_hit, local_tile[:, :, None], 1)
+        ending = listed & (list_home.reshape(-1, 1) == me) & (middle == device_ids)
+        last = choose(ending, (term_list // tag - me * span).reshape(-1, 1), 0)
+        return scatter_terms(landing, arrived, rows_dev, blocks, last, relayed)
+
+    def write_one_step():
+        slots = slot_count(most)
+        wide = slot_count(2 * slots)
+        places = rank[:, None, None] == jnp.arange(slots)
+        term_of_slot = choose(to_holder[:, :, None] & places, tile_ids[:, None, None], 0)
+        none = jnp.full((devices, wide // 2 - slots), -1, jnp.int32)
+        low_term = jnp.where(term_of_slot >= 0, term_of_slot + tile_count, -1)
+        arrived = send(jnp.concatenate([term_of_slot, none, low_term, none], axis=1), wide)
+        wanted = requests(slots)
+        landing = jnp.concatenate([wanted, none, wanted, none], axis=1)
+        return scatter_terms(landing, arrived, rows_dev, blocks)
+
+    fock = lax.cond(term_fits, write_two_step, write_one_step)
     return jnp.transpose(fock, (0, 2, 1, 3))
 
 

time: 537 us -> 337 us (0.63)
  waiting for transfers between devices: 376 us -> 117 us
  local copies, waits for them, and re-layouts: 7.47 us -> 25.2 us
  Pallas kernels: 133 us -> 143 us
  loops' own time: 0 us -> 9.99 us
  starting transfers between devices: 14.7 us -> 22.9 us
  other arithmetic: 5.48 us -> 11.9 us
    all_to_all x3 -> x5, waiting for transfers between devices: 376 us -> 117 us  [exchange_slots(): lax.all_to_all(array, AXES, split_axis=axis, concat_axis=axis, tiled=True)]
    pallas_call x2 -> x6, Pallas kernels: 26.2 us -> 55.5 us  [the longest x2 24.8 us: route(): pl.pallas_call(functools.partial(route_body, peers=peers, spare=spare, sc...]
    pallas_call x1, Pallas kernels: 27.8 us -> 10.3 us  [pack_terms(): pl.pallas_call(pack_body, grid=(count // chunk,), in_specs=[pl.BlockSpec(...]
    reshape x1 -> x15, local copies, waits for them, and re-layouts: 0.08 us -> 13.3 us  [the longest x4 5.66 us: relay(): got = exchange_slots(sent.reshape(groups, peers, RELAY_ROWS, lanes), 1)]
    unnamed x0 -> x1, loops' own time: none -> 9.58 us
    all_to_all x3 -> x5, starting transfers between devices: 14.7 us -> 22.9 us  [exchange_slots(): lax.all_to_all(array, AXES, split_axis=axis, concat_axis=axis, tiled=True)]
  transfers between devices with their start and end apart: 3 -> 5, of which waited for: 3 -> 5; matrix products, arithmetic and copies ran while one was open for 2% -> 5% of each run, Pallas kernels for 8% -> 17%
where the time goes in v2:
time: 337 us; the launch traced here: 333 us
  Pallas kernels  143 us (42%)
  waiting for transfers between devices  117 us (35%)
  local copies, waits for them, and re-layouts  25.2 us (7%)
  starting transfers between devices  22.9 us (7%)
  other arithmetic  11.9 us (4%)
  loops' own time  9.99 us (3%)
    all_to_all x5, waiting for transfers between devices, exchange_slots(): lax.all_to_all(array, AXES, split_axis=axis, concat_axis=axis, tiled=True)  117 us
    pallas_call x1, Pallas kernels, regroup(): pl.pallas_call(functools.partial(regroup_body, width=width), grid=(count,...  40.9 us
    pallas_call x1, Pallas kernels, contract(): pl.pallas_call(contract_body, grid=(count,), in_specs=[part, whole, whole...  25.7 us
    pallas_call x2, Pallas kernels, route(): pl.pallas_call(functools.partial(route_body, peers=peers, spare=spare, sc...  24.8 us
    all_to_all x5, starting transfers between devices, exchange_slots(): lax.all_to_all(array, AXES, split_axis=axis, concat_axis=axis, tiled=True)  22.9 us
    pallas_call x3, Pallas kernels, pick_rows(): pl.pallas_call(functools.partial(pick_body, relay=relayed is not None, sw...  16.6 us
    pallas_call x1, Pallas kernels, scatter_terms(): pl.pallas_call(functools.partial(scatter_body, relay=relayed is not None)...  14.1 us
    pallas_call x1, Pallas kernels, gather_tiles(): pl.pallas_call(gather_body, grid=(groups,), in_specs=[pl.BlockSpec((peers...  10.9 us
  transfers between devices with their start and end apart: 5, of which 5 were waited for; matrix products, arithmetic and copies ran while one was open for 5% of the time, Pallas kernels for 17%

profile of v2, /device:TPU:0, one launch (start us, length us, event | category | flops | bytes accessed | tf_op | source)
XLA Modules:
  0.0 332.9 jit_solution(17037375349769636859)
XLA Ops:
  4.3 7.3 %all-to-all-start.6 = ((s32[32,1,128]{2,1,0:T(1,128)}), s32[32,1,128]{2,1,0:T(1,128)S(1)}, u32[]{:S(2)}, u32[]{:S(2)}) async-start(s32[32,1,128]{2,1,0:T(1,128)} %broadcast_in_dim.436), calls=%async_computation.6 | async-start | bytes 32768 | tf_op jit(solution)/shard_map/all_to_all | solution.py:489
  12.8 6.0 %all-to-all-done.6 = s32[32,1,128]{2,1,0:T(1,128)S(1)} async-done(((s32[32,1,128]{2,1,0:T(1,128)}), s32[32,1,128]{2,1,0:T(1,128)S(1)}, u32[]{:S(2)}, u32[]{:S(2)}) %all-to-all-start.6) | async-done | bytes 16416 | tf_op jit(solution)/shard_map/all_to_all | solution.py:489
  21.0 8.7 %route.5 = s32[257]{0:T(512)S(1)} custom-call(s32[256]{0:T(256)} %reshape.1511.list_ref, s32[2048]{0:T(1024)} %reshape.1512.state_hbm), custom_call_target="tpu_custom_call" | custom-call | tf_op jit(solution)/shard_map/route/pallas_call | solution.py:419
  31.6 138.9 %conditional.5 = (bf16[8,1024,1024]{2,1,0:T(8,128)(2,1)}, bf16[8,1024,1024]{2,1,0:T(8,128)(2,1)}, s32[32,48]{1,0:T(8,128)S(1)}, s32[32,16]{1,0:T(8,128)S(1)}, s3...) conditional(s32[]{:T(128)} %convert_element_type.77, ...), branch_computations={%region_7.16_spmd, %region_16.28_spmd} | conditional | flops 34368745472 | bytes 69518648
  41.3 10.9 %gather_tiles.3 = bf16[32,3,16,1024]{3,2,1,0:T(8,128)(2,1)} custom-call(s32[512,1]{1,0:T(8,128)} %select_n.623.target_ref, bf16[4,12,128,1024]{3,2,1,0:T(8,128)(2,1)} %get-tuple-element.178.density_ref), custom_call_target="tpu_custom_call" | custom-call | tf_op jit(solution)/shard_map/cond/branch_1_fun/gather_tiles/pallas_call | solution.py:102
  52.1 3.5 %all-to-all-start.4 = ((bf16[32,3,16,1024]{3,2,1,0:T(8,128)(2,1)}), bf16[32,3,16,1024]{3,2,1,0:T(8,128)(2,1)}, u32[]{:S(2)}, u32[]{:S(2)}) async-start(bf16[32,3,16,1024]{3,2,1,0:T(8,128)(2,1)} %gather_tiles.3), calls=%async_computation.4 | async-start | bytes 6291456 | tf_op jit(solution)/shard_map/cond/branch_1_fun/all_to_all | solution.py:489
  61.1 16.1 %route.4 = s32[513]{0:T(1024)} custom-call(s32[512]{0:T(512)} %sub.153.list_ref, s32[2048]{0:T(1024)} %reshape.1490.state_hbm), custom_call_target="tpu_custom_call" | custom-call | tf_op jit(solution)/shard_map/cond/branch_1_fun/route/pallas_call | solution.py:419
  79.4 40.9 %regroup.3 = (bf16[8,1024,1024]{2,1,0:T(8,128)(2,1)}, bf16[8,1024,1024]{2,1,0:T(8,128)(2,1)}) custom-call(bf16[1024,1024]{1,0:T(8,128)(2,1)S(1)} %get-tuple-element.179.refs_2_, bf16[512,512]{1,0:T(8,128)(2,1)S(1)} %get-tuple-element.160.trade_ref, bf16[8,1024,1024]{2,1,0:T(8,128)(2,1)} %get-tuple-element.161.block_ref), custom_call_target="tpu_custom_call" | custom-call | flops 34359738368 | bytes 50331648 | tf_op jit(solution)/shard_map/cond/branch_1_fun/regroup/pallas_call | solution.py:227
  120.2 6.9 %all-to-all-done.4 = bf16[32,3,16,1024]{3,2,1,0:T(8,128)(2,1)} async-done(((bf16[32,3,16,1024]{3,2,1,0:T(8,128)(2,1)}), bf16[32,3,16,1024]{3,2,1,0:T(8,128)(2,1)}, u32[]{:S(2)}, u32[]{:S(2)}) %all-to-all-start.4) | async-done | bytes 3145760 | tf_op jit(solution)/shard_map/cond/branch_1_fun/all_to_all | solution.py:489
  127.1 4.8 %pick_rows.5 = bf16[384,1024]{1,0:T(8,128)(2,1)} custom-call(s32[384,1]{1,0:T(8,128)} %select_n.622.refs_0_, bf16[1536,1024]{1,0:T(8,128)(2,1)} %bitcast.4.refs_1_.refs_4_), custom_call_target="tpu_custom_call" | custom-call | tf_op jit(solution)/shard_map/cond/branch_1_fun/pick_rows/pallas_call | solution.py:162
  131.9 1.7 reshape.1495
  134.7 4.1 %all-to-all-start.5 = ((bf16[3,32,4,1024]{3,2,0,1:T(4,128)(2,1)}), bf16[3,32,4,1024]{3,2,0,1:T(4,128)(2,1)S(1)}, u32[]{:S(2)}, u32[]{:S(2)}) async-start(bf16[3,32,4,1024]{3,2,0,1:T(4,128)(2,1)} %copy.36), calls=%async_computation.5 | async-start | bytes 1572864 | tf_op jit(solution)/shard_map/cond/branch_1_fun/all_to_all | solution.py:489
  143.0 16.4 %all-to-all-done.5 = bf16[3,32,4,1024]{3,2,0,1:T(4,128)(2,1)S(1)} async-done(((bf16[3,32,4,1024]{3,2,0,1:T(4,128)(2,1)}), bf16[3,32,4,1024]{3,2,0,1:T(4,128)(2,1)S(1)}, u32[]{:S(2)}, u32[]{:S(2)}) %all-to-all-start.5) | async-done | bytes 786464 | tf_op jit(solution)/shard_map/cond/branch_1_fun/all_to_all | solution.py:489
  160.6 2.3 reshape.1496.refs_1_
  162.9 7.1 %pick_rows.6 = bf16[768,1024]{1,0:T(8,128)(2,1)S(1)} custom-call(s32[768,1]{1,0:T(8,128)} %reshape.1516.refs_0_, bf16[384,1024]{1,0:T(8,128)(2,1)} %reshape.1496.refs_1_, bf16[1024,1024]{1,0:T(8,128)(2,1)S(1)} %get-tuple-element.179.refs_2_, s32[768,1]{1,0:T(8,128)} %reshape.1517.refs_3_, bf16[1536,1024]{1,0:T(8,128)(2,1)} %bitcast.4.refs_1_.refs_4_), custom_call_target="tpu_custom_call" | custom-call | tf_op jit(solution)/shard_map/cond/branch_1_fun/pick_rows/pallas_call | solution.py:162
  170.4 25.7 %contract.1 = (bf16[6,8,16,1024]{3,2,1,0:T(8,128)(2,1)}, bf16[6,8,16,1024]{3,2,1,0:T(8,128)(2,1)}) custom-call(bf16[6,8,16,1024]{3,2,1,0:T(8,128)(2,1)S(1)} %get-tuple-element.219.tiles_ref, bf16[8,1024,1024]{2,1,0:T(8,128)(2,1)} %block_ref.1, bf16[8,1024,1024]{2,1,0:T(8,128)(2,1)} %get-tuple-element.220.first_ref, ...), custom_call_target="tpu_custom_call" | custom-call | tf_op jit(solution)/shard_map/contract/pallas_call | solution.py:268
  196.2 135.7 %conditional.4 = (bf16[4,12,128,1024]{3,2,1,0:T(8,128)(2,1)}) conditional(s32[]{:T(128)} %get-tuple-element.244, (pred[32,48]{1,0:T(8,128)(4,1)S(1)}, s32[32,48]{1,0:T(8,128)S(1)}, s32[32,48]{1,0:T(8,128)S(1)}, pred[48,32]{0,1:T(8,128)(4,1)S(1)}, s32[48]{0:T(128)S(1)}, /*index=5*/s32[48]{0:T(128)S(1)}, bf16[1024,1024]{1,0:T(8,128)(2,1)S(1)}, ...), branch_computations={%region_28.31_spmd, %region_31.37_spmd} | conditional | flops 262480 | bytes 37879336 | solution.py:654
  198.4 10.3 %pack_terms.3 = bf16[1536,1024]{1,0:T(8,128)(2,1)} custom-call(s32[1536,1]{1,0:T(8,128)} %select_n.626.target_ref, bf16[1024,1024]{1,0:T(8,128)(2,1)S(1)} %get-tuple-element.201.swap_ref, bf16[768,1024]{1,0:T(8,128)(2,1)} %get-tuple-element.202.high_ref, bf16[768,1024]{1,0:T(8,128)(2,1)} %get-tuple-element.203.low_ref), custom_call_target="tpu_custom_call" | custom-call | tf_op jit(solution)/shard_map/cond/branch_1_fun/pack_terms/pallas_call | solution.py:300
  208.7 3.9 %all-to-all-start.1 = ((bf16[32,3,16,1024]{3,2,1,0:T(8,128)(2,1)}), bf16[32,3,16,1024]{3,2,1,0:T(8,128)(2,1)}, u32[]{:S(2)}, u32[]{:S(2)}) async-start(bf16[32,3,16,1024]{3,2,1,0:T(8,128)(2,1)} %bitcast.47), calls=%async_computation.1 | async-start | bytes 6291456 | tf_op jit(solution)/shard_map/cond/branch_1_fun/all_to_all | solution.py:489
  214.6 69.4 %all-to-all-done.1.refs_3_ = bf16[32,3,16,1024]{3,2,1,0:T(8,128)(2,1)} async-done(((bf16[32,3,16,1024]{3,2,1,0:T(8,128)(2,1)}), bf16[32,3,16,1024]{3,2,1,0:T(8,128)(2,1)}, u32[]{:S(2)}, u32[]{:S(2)}) %all-to-all-start.1) | async-done | bytes 3145760 | tf_op jit(solution)/shard_map/cond/branch_1_fun/all_to_all | solution.py:489
  284.0 4.8 %pick_rows.7 = bf16[384,1024]{1,0:T(8,128)(2,1)} custom-call(s32[384,1]{1,0:T(8,128)} %select_n.625.refs_0_, bf16[1536,1024]{1,0:T(8,128)(2,1)} %bitcast.13.refs_1_), custom_call_target="tpu_custom_call" | custom-call | tf_op jit(solution)/shard_map/cond/branch_1_fun/pick_rows/pallas_call | solution.py:162
  291.6 4.0 %all-to-all-start.2 = ((bf16[3,32,4,1024]{3,2,0,1:T(4,128)(2,1)}), bf16[3,32,4,1024]{3,2,0,1:T(4,128)(2,1)S(1)}, u32[]{:S(2)}, u32[]{:S(2)}) async-start(bf16[3,32,4,1024]{3,2,0,1:T(4,128)(2,1)} %copy.46), calls=%async_computation.2 | async-start | bytes 1572864 | tf_op jit(solution)/shard_map/cond/branch_1_fun/all_to_all | solution.py:489
  297.7 18.5 %all-to-all-done.2 = bf16[3,32,4,1024]{3,2,0,1:T(4,128)(2,1)S(1)} async-done(((bf16[3,32,4,1024]{3,2,0,1:T(4,128)(2,1)}), bf16[3,32,4,1024]{3,2,0,1:T(4,128)(2,1)S(1)}, u32[]{:S(2)}, u32[]{:S(2)}) %all-to-all-start.2) | async-done | bytes 786464 | tf_op jit(solution)/shard_map/cond/branch_1_fun/all_to_all | solution.py:489
  317.6 14.1 %scatter_terms.3 = bf16[4,12,128,1024]{3,2,1,0:T(8,128)(2,1)} custom-call(s32[1,128]{1,0:T(1,128)} %add_select_fusion.29.refs_0_, bf16[3,128,1024]{2,1,0:T(8,128)(2,1)} %reshape.1504.refs_1_, s32[1,512]{1,0:T(1,128)} %select_n.582.refs_2_, bf16[32,3,16,1024]{3,2,1,0:T(8,128)(2,1)} %all-to-all-done.1.refs_3_), custom_call_target="tpu_custom_call" | custom-call | tf_op jit(solution)/shard_map/cond/branch_1_fun/scatter_terms/pallas_call | solution.py:355
  (171 shorter events, 33.2 us)
Async XLA Ops:
  4.3 14.4 %all-to-all-start.6 = ((s32[32,1,128]{2,1,0:T(1,128)}), s32[32,1,128]{2,1,0:T(1,128)S(1)}, u32[]{:S(2)}, u32[]{:S(2)}) async-start(s32[32,1,128]{2,1,0:T(1,128)} %broadcast_in_dim.436), calls=%async_computation.6 | async-start | bytes 32768 | tf_op jit(solution)/shard_map/all_to_all | solution.py:489
  52.1 75.0 %all-to-all-start.4 = ((bf16[32,3,16,1024]{3,2,1,0:T(8,128)(2,1)}), bf16[32,3,16,1024]{3,2,1,0:T(8,128)(2,1)}, u32[]{:S(2)}, u32[]{:S(2)}) async-start(bf16[32,3,16,1024]{3,2,1,0:T(8,128)(2,1)} %gather_tiles.3), calls=%async_computation.4 | async-start | bytes 6291456 | tf_op jit(solution)/shard_map/cond/branch_1_fun/all_to_all | solution.py:489
  57.5 62.7 %copy-start.2 = (s32[32,48]{1,0:T(8,128)}, s32[32,48]{1,0:T(8,128)S(1)}, u32[]{:S(2)}) copy-start(s32[32,48]{1,0:T(8,128)S(1)} %broadcast_select_fusion.1) | copy-start | bytes 18436
  59.1 61.2 %copy-start = (s32[32,16]{1,0:T(8,128)}, s32[32,16]{1,0:T(8,128)S(1)}, u32[]{:S(2)}) copy-start(s32[32,16]{1,0:T(8,128)S(1)} %broadcast_add_fusion.4) | copy-start | bytes 6148
  120.2 22.7 %slice-start = ((s32[513]{0:T(1024)}), s32[512]{0:T(512)S(1)}, s32[]{:S(2)}) async-start(s32[513]{0:T(1024)} %route.4), calls=%async_computation.7 | async-start | bytes 4096 | tf_op jit(solution)/shard_map/cond/branch_1_fun/slice | solution.py:429
  134.7 24.7 %all-to-all-start.5 = ((bf16[3,32,4,1024]{3,2,0,1:T(4,128)(2,1)}), bf16[3,32,4,1024]{3,2,0,1:T(4,128)(2,1)S(1)}, u32[]{:S(2)}, u32[]{:S(2)}) async-start(bf16[3,32,4,1024]{3,2,0,1:T(4,128)(2,1)} %copy.36), calls=%async_computation.5 | async-start | bytes 1572864 | tf_op jit(solution)/shard_map/cond/branch_1_fun/all_to_all | solution.py:489
  138.9 31.1 %copy-start.1 = (s32[32,16]{1,0:T(8,128)S(1)}, s32[32,16]{1,0:T(8,128)}, u32[]{:S(2)}) copy-start(s32[32,16]{1,0:T(8,128)} %copy-done) | copy-start | bytes 6148
  138.9 31.1 %copy-start.3 = (s32[32,48]{1,0:T(8,128)S(1)}, s32[32,48]{1,0:T(8,128)}, u32[]{:S(2)}) copy-start(s32[32,48]{1,0:T(8,128)} %copy-done.2) | copy-start | bytes 18436
  208.7 75.3 %all-to-all-start.1 = ((bf16[32,3,16,1024]{3,2,1,0:T(8,128)(2,1)}), bf16[32,3,16,1024]{3,2,1,0:T(8,128)(2,1)}, u32[]{:S(2)}, u32[]{:S(2)}) async-start(bf16[32,3,16,1024]{3,2,1,0:T(8,128)(2,1)} %bitcast.47), calls=%async_computation.1 | async-start | bytes 6291456 | tf_op jit(solution)/shard_map/cond/branch_1_fun/all_to_all | solution.py:489
  291.6 24.6 %all-to-all-start.2 = ((bf16[3,32,4,1024]{3,2,0,1:T(4,128)(2,1)}), bf16[3,32,4,1024]{3,2,0,1:T(4,128)(2,1)S(1)}, u32[]{:S(2)}, u32[]{:S(2)}) async-start(bf16[3,32,4,1024]{3,2,0,1:T(4,128)(2,1)} %copy.46), calls=%async_computation.2 | async-start | bytes 1572864 | tf_op jit(solution)/shard_map/cond/branch_1_fun/all_to_all | solution.py:489
